TPU v7x, 32 devices: a whole 2x2x4 slice. The times are simulated.
32 devices in a mesh: beam: 2 (over x), wide: 16 (over z, y, core).
Axes of the slice: x: 2, y: 2, z: 4, core: 2. Of those that a mesh axis runs over, the one named last changes fastest.
Arguments:
- filterbank: bfloat16 [2, 4096, 4096], P('beam', 'wide'), parts along dimension 0, may hold values from -100 to 100
- channel_mask: int32 [8192], P(('beam', 'wide')), parts along dimension 0, may hold values 0 or 1
- band_edges: int32 [7], replicated, may hold values from 385 to 3711, as said below
- dm_delays: int32 [16], replicated, may hold values from 0 to 2047
Outputs:
- series: float32 [2, 16, 4096], P('beam', 'wide'), parts along dimension 0
There are 2 independent parts, one for each index of `beam`. A program takes and returns all parts, laid end to end along the dimension named above; an argument that names none is the same for every part. Nothing has to cross between parts.
Inputs may be any that keep to these rules, and one draw needn't show every extreme that they name: `band_edges`: strictly increasing; entry i lies at (i + 1) * 512 up to a shift of less than 128.
All inputs are finite; a program needn't handle non-finite values. No bound on the sum of `channel_mask` on one device may be relied on, other than what follows from the above.
Results may differ from a plain program's by a relative error of at most 0.0063.
Values may be sent and summed in bfloat16 or wider, within the bound.
A program may use at most 64 MiB of HBM per device.

v0:
```python
import functools
import math

import jax
import jax.numpy as jnp
import numpy as np
from jax import lax
from jax.experimental import pallas as pl
from jax.experimental.pallas import tpu as pltpu
from jax.sharding import PartitionSpec as P

NBLK = 8
LANES = 128
VMEM = pl.BlockSpec(memory_space=pltpu.VMEM)
SMEM = pl.BlockSpec(memory_space=pltpu.SMEM)
MESH = pl.DeviceIdType.MESH
HIGH = lax.Precision.HIGHEST


def turn_coefficients():
    degree = 5
    nodes = np.cos((np.arange(64) + 0.5) * np.pi / 64) * 0.125 + 0.125
    root = np.sqrt(nodes)
    cos_fit = np.polynomial.Chebyshev.fit(nodes, np.cos(2 * np.pi * root), degree, domain=[0, 0.25])
    sin_fit = np.polynomial.Chebyshev.fit(
        nodes, np.sin(2 * np.pi * root) / root, degree, domain=[0, 0.25]
    )
    as_power = lambda fit: [float(np.float32(v)) for v in fit.convert(kind=np.polynomial.Polynomial).coef]
    return as_power(cos_fit), as_power(sin_fit)


COS_COEF, SIN_COEF = turn_coefficients()


def cos_sin_turns(turns):
    r = turns - jnp.floor(turns + 0.5)
    s = r * r
    c = jnp.full_like(s, COS_COEF[-1])
    q = jnp.full_like(s, SIN_COEF[-1])
    for a, b in zip(COS_COEF[-2::-1], SIN_COEF[-2::-1]):
        c = c * s + a
        q = q * s + b
    return c, q * r


def forward_seeds(samples):
    fine = 32
    quarter = samples // 4
    f = (8 * np.arange(quarter // 8)[None, :] + np.arange(8)[:, None]).reshape(-1)
    coarse = (np.arange(samples // 8 // fine) * fine)[:, None] * f[None, :] % samples
    small = np.arange(fine)[:, None] * f[None, :] % samples
    out = []
    for product in (coarse, small):
        angle = product * (2 * np.pi / samples)
        out += [np.cos(angle), np.sin(angle)]
    return [v.astype(np.float32) for v in out]


def inverse_seeds(samples, channels):
    lane = np.arange(LANES)
    f = 8 * lane[None, :] + np.arange(8)[:, None]
    weight = np.where(f == 0, 1.0, 2.0) / (samples * math.sqrt(channels))
    angle = (f[:, :, None] * np.arange(LANES)[None, None, :] % samples) * (2 * np.pi / samples)
    first = [weight[:, :, None] * np.cos(angle), weight[:, :, None] * np.sin(angle)]
    steps = samples // LANES
    b = f
    turn = (b[:, None, :] * np.arange(steps)[None, :, None] % steps) * (2 * np.pi / steps)
    second = np.stack([np.cos(turn), -np.sin(turn)], axis=1).reshape(16, steps, LANES)
    second = np.concatenate(list(second), axis=1)
    return [v.astype(np.float32) for v in first + [second]]


def member_rows(edges_ref, channel, bands, channels):
    rows = []
    for j in range(bands):
        inside = channel < (channels if j == bands - 1 else edges_ref[j])
        if j:
            inside = jnp.logical_and(inside, channel >= edges_ref[j - 1])
        rows.append(inside)
    return rows


def partner(me, step, n):
    if n & (n - 1):
        return lax.rem(me + step, n)
    out, bit = 0, 1
    while bit < n:
        out = out + lax.rem(me // bit + step // bit, 2) * bit
        bit *= 2
    return out


def fused_kernel(
    n, bands, channels, trials,
    edges_ref, delays_ref, mask_ref, x_hbm, ac_ref, as_ref, bc_ref, bs_ref,
    out_ref,
    x_ref, acc_ref, tab_ref, y_ref, spec_re, spec_im, rot_ref, base_ref, frac_ref,
    own_power, got_power, part_ref, got_part,
    x_sem, power_send, power_recv, part_send, part_recv,
):
    local, samples = x_ref.shape
    quarter = samples // 4
    window = samples // NBLK
    eighth = samples // 8
    group = quarter // 8
    assert group == LANES and eighth == window
    share = out_ref.shape[0]
    fine = bc_ref.shape[0]
    me = lax.axis_index("wide")
    first = me * local

    barrier = pltpu.get_barrier_semaphore()
    for step in range(1, n):
        pl.semaphore_signal(
            barrier, inc=1, device_id={"wide": lax.rem(me + step, n)}, device_id_type=MESH
        )

    rows = 64

    def load(i):
        at = pl.ds(pl.multiple_of(i * rows, rows), rows)
        return pltpu.make_async_copy(x_hbm.at[at], x_ref.at[at], x_sem.at[i])

    for i in range(local // rows):
        load(i).start()

    def fill(i, carry):
        at = pl.ds(pl.multiple_of(i * fine, fine), fine)
        ca, sa = ac_ref[pl.ds(i, 1), :], as_ref[pl.ds(i, 1), :]
        cb, sb = bc_ref[...], bs_ref[...]
        cos_part = (ca * cb - sa * sb).astype(jnp.bfloat16)
        sin_part = (sa * cb + ca * sb).astype(jnp.bfloat16)
        for r in range(8):
            tab_ref[at, 2 * r * group : (2 * r + 1) * group] = cos_part[:, r * group : (r + 1) * group]
            tab_ref[at, (2 * r + 1) * group : (2 * r + 2) * group] = sin_part[:, r * group : (r + 1) * group]
        return carry

    lax.fori_loop(0, eighth // fine, fill, 0)

    def square(i, carry):
        load(i).wait()
        at = pl.ds(pl.multiple_of(i * rows, rows), rows)
        for k in range(NBLK):
            total = None
            for p in range(window // LANES):
                v = x_ref[at, pl.ds(k * window + p * LANES, LANES)].astype(jnp.float32)
                total = v * v if total is None else total + v * v
            acc_ref[at, pl.ds(k * LANES, LANES)] = total
        return carry

    lax.fori_loop(0, local // rows, square, 0)
    channel_row = first + lax.broadcasted_iota(jnp.int32, (1, local), 1)
    keep = mask_ref[...].astype(jnp.float32)
    picks = [jnp.where(m, keep, 0.0) for m in member_rows(edges_ref, channel_row, bands, channels)]
    pick = jnp.concatenate(picks, axis=0)
    summed = jnp.dot(pick, acc_ref[...], precision=HIGH, preferred_element_type=jnp.float32)
    spot = lax.broadcasted_iota(jnp.int32, (bands, LANES), 1)
    powers = jnp.zeros((bands, LANES), jnp.float32)
    for k in range(NBLK):
        part = jnp.sum(summed[:, k * LANES : (k + 1) * LANES], axis=1, keepdims=True)
        powers = jnp.where(spot == k, part / window, powers)
    own_power[...] = powers

    channel = first + lax.broadcasted_iota(jnp.int32, (local, LANES), 0)
    ratio = 0.5 + 0.5 * (channel.astype(jnp.float32) + 0.5) / channels
    fraction = (1.0 / (ratio * ratio) - 1.0) / 3.0
    frac_ref[...] = fraction
    lane = lax.broadcasted_iota(jnp.int32, (1, LANES), 1)
    delay_row = jnp.zeros((1, LANES), jnp.float32)
    for d in range(trials):
        delay_row = jnp.where(lane == d, delays_ref[d].astype(jnp.float32), delay_row)
    sweep = fraction * (delay_row * (1.0 / samples))
    rotations = cos_sin_turns(sweep)

    pl.semaphore_wait(barrier, n - 1)
    power_copies = []
    for step in range(1, n):
        copy = pltpu.make_async_remote_copy(
            src_ref=own_power,
            dst_ref=got_power.at[step],
            send_sem=power_send.at[step],
            recv_sem=power_recv.at[step],
            device_id={"wide": lax.rem(me + step, n)},
            device_id_type=MESH,
        )
        copy.start()
        power_copies.append(copy)

    for d in range(trials):
        for i, rot in enumerate(rotations):
            rot_ref[d, i] = jnp.broadcast_to(rot[:, d : d + 1], (local, LANES))

    def base(d, carry):
        delay = delays_ref[d].astype(jnp.float32) * (1.0 / samples)
        per_lane = lane_step * delay

        def tile(i, inner):
            at = pl.ds(pl.multiple_of(i * 8, 8), 8)
            base_ref[d, 0, at, :], base_ref[d, 1, at, :] = cos_sin_turns(frac_ref[at, :] * per_lane)
            return inner

        return lax.fori_loop(0, local // 8, tile, carry, unroll=8)

    lane_step = lax.broadcasted_iota(jnp.int32, (8, LANES), 1).astype(jnp.float32) * 8.0
    lax.fori_loop(0, trials, base, 0)

    band_power = own_power[...]
    for step in range(1, n):
        power_copies[step - 1].wait()
        band_power = band_power + got_power[step]

    scale = jnp.zeros((local, LANES), jnp.float32)
    members = member_rows(edges_ref, channel, bands, channels)
    for j in range(bands):
        high = channels if j == bands - 1 else edges_ref[j]
        low = edges_ref[j - 1] if j else 0
        width = jnp.full((1, LANES), high - low, jnp.int32).astype(jnp.float32)
        level = 1.0 / jnp.sqrt(band_power[j : j + 1, :] / width + 1e-05)
        scale = jnp.where(members[j], level, scale)
    scale = scale * jnp.transpose(jnp.broadcast_to(keep, (LANES, local)))

    columns = [scale[:, m : m + 1] for m in range(8)]
    root = math.sqrt(0.5)
    for p in range(window // LANES):
        here = slice(p * LANES, (p + 1) * LANES)
        x = [
            x_ref[:, m * window + p * LANES : m * window + (p + 1) * LANES].astype(jnp.float32)
            * columns[m]
            for m in range(8)
        ]
        plus = [x[m] + x[m + 4] for m in range(4)]
        minus = [x[m] - x[m + 4] for m in range(4)]
        even, odd = plus[0] + plus[2], plus[1] + plus[3]
        near, far = root * (minus[1] - minus[3]), root * (minus[1] + minus[3])
        folded = (
            even + odd, even - odd,
            minus[0] + near, -(far + minus[2]),
            plus[0] - plus[2], plus[3] - plus[1],
            minus[0] - near, minus[2] - far,
        )
        for i, value in enumerate(folded):
            y_ref[i, :, here] = value.astype(jnp.bfloat16)

    def product(which, r):
        both = jnp.dot(
            y_ref[which], tab_ref[:, 2 * r * group : (2 * r + 2) * group],
            preferred_element_type=jnp.float32,
        )
        return both[:, :group], both[:, group:]

    for r in range(8):
        to = slice(r * group, (r + 1) * group)
        if r % 4 == 0:
            c, q = product(r // 4, r)
            spec_re[:, to], spec_im[:, to] = c, -q
        else:
            kind = min(r, 8 - r)
            (a_c, a_s), (b_c, b_s) = product(2 * kind, r), product(2 * kind + 1, r)
            if r < 4:
                spec_re[:, to], spec_im[:, to] = a_c + b_s, b_c - a_s
            else:
                spec_re[:, to], spec_im[:, to] = a_c - b_s, -(b_c + a_s)

    blocks = 8
    early = max(1, local // 32)

    def part_copy(step):
        return pltpu.make_async_remote_copy(
            src_ref=part_ref.at[step],
            dst_ref=got_part.at[step],
            send_sem=part_send.at[step],
            recv_sem=part_recv.at[step],
            device_id={"wide": partner(me, step, n)},
            device_id_type=MESH,
        )

    def owner_step(turn, carry):
        step = n - 1 - turn
        owner = partner(me, step, n)
        for sub in range(share):
            d = owner * share + sub

            def rotate(i, totals):
                at = pl.ds(pl.multiple_of(i * 8, 8), 8)
                base_re, base_im = base_ref[d, 0, at, :], base_ref[d, 1, at, :]
                one_re, one_im = rot_ref[d, 0, at, :], rot_ref[d, 1, at, :]
                twice = one_re + one_re
                totals = list(totals)
                phases = [
                    (base_re, base_im),
                    (base_re * one_re - base_im * one_im, base_re * one_im + base_im * one_re),
                ]
                for r in range(8):
                    if r > 1:
                        (b_re, b_im), (a_re, a_im) = phases[-2:]
                        phases.append((twice * a_re - b_re, twice * a_im - b_im))
                    e_re, e_im = phases[r]
                    col = pl.ds(r * LANES, LANES)
                    s_re, s_im = spec_re[at, col], spec_im[at, col]
                    totals[r] = totals[r] + (s_re * e_re - s_im * e_im)
                    totals[blocks + r] = totals[blocks + r] + (s_re * e_im + s_im * e_re)
                return tuple(totals)

            zero = jnp.zeros((8, LANES), jnp.float32)
            totals = lax.fori_loop(0, early, rotate, (zero,) * (2 * blocks), unroll=8)
            if sub == 0:

                @pl.when(turn > 0)
                def _():
                    part_copy(step + 1).start()

            totals = lax.fori_loop(early, local // 8, rotate, totals, unroll=8)
            part_ref[step, sub] = jnp.concatenate(
                [jnp.sum(v, axis=0, keepdims=True) for v in totals], axis=0
            )
        return carry

    lax.fori_loop(0, n, owner_step, 0)
    total = part_ref[0]
    for step in range(n - 1, 0, -1):
        part_copy(step).wait()
        total = total + got_part[step]
    out_ref[...] = total


def series_kernel(x_ref, fc_ref, fs_ref, g_ref, out_ref):
    blocks = fc_ref.shape[0]
    for b in range(x_ref.shape[0]):
        rounded = x_ref[b].astype(jnp.bfloat16).astype(jnp.float32)
        turned = jnp.transpose(rounded)
        parts = []
        for k in range(blocks):
            d_re, d_im = turned[:, k : k + 1], turned[:, blocks + k : blocks + k + 1]
            parts += [d_re * fc_ref[k] - d_im * fs_ref[k], d_re * fs_ref[k] + d_im * fc_ref[k]]
        out_ref[b] = jnp.dot(
            g_ref[...], jnp.concatenate(parts, axis=0),
            precision=HIGH, preferred_element_type=jnp.float32,
        )


def body(n, filterbank, channel_mask, band_edges, dm_delays):
    beams, local, samples = filterbank.shape
    channels = local * n
    bands = band_edges.shape[0] + 1
    trials = dm_delays.shape[0]
    share = trials // n
    quarter = samples // 4
    blocks = quarter // LANES
    steps = samples // LANES
    ac, as_, bc, bs = forward_seeds(samples)
    fc, fs, g = inverse_seeds(samples, channels)
    x = filterbank.reshape(local, samples)

    slot = (share, 2 * blocks, LANES)
    dma = pltpu.SemaphoreType.DMA((n,))
    summed = pl.pallas_call(
        functools.partial(fused_kernel, n, bands, channels, trials),
        out_shape=jax.ShapeDtypeStruct(slot, jnp.float32),
        in_specs=[SMEM, SMEM, VMEM, pl.BlockSpec(memory_space=pl.ANY)] + [VMEM] * 4,
        out_specs=VMEM,
        scratch_shapes=[
            pltpu.VMEM((local, samples), x.dtype),
            pltpu.VMEM((local, NBLK * LANES), jnp.float32),
            pltpu.VMEM((samples // 8, 2 * quarter), jnp.bfloat16),
            pltpu.VMEM((8, local, samples // 8), jnp.bfloat16),
            pltpu.VMEM((local, quarter), jnp.float32),
            pltpu.VMEM((local, quarter), jnp.float32),
            pltpu.VMEM((trials, 2, local, LANES), jnp.float32),
            pltpu.VMEM((trials, 2, local, LANES), jnp.float32),
            pltpu.VMEM((local, LANES), jnp.float32),
            pltpu.VMEM((bands, LANES), jnp.float32),
            pltpu.VMEM((n, bands, LANES), jnp.float32),
            pltpu.VMEM((n,) + slot, jnp.float32),
            pltpu.VMEM((n,) + slot, jnp.float32),
            pltpu.SemaphoreType.DMA((local // 64,)), dma, dma, dma, dma,
        ],
        compiler_params=pltpu.CompilerParams(collective_id=0, has_side_effects=True),
    )(band_edges, dm_delays, channel_mask.reshape(1, local), x, ac, as_, bc, bs)
    series = pl.pallas_call(
        series_kernel,
        out_shape=jax.ShapeDtypeStruct((share, steps, LANES), jnp.float32),
        in_specs=[VMEM] * 4,
        out_specs=VMEM,
    )(summed, fc, fs, g)
    return series.reshape(beams, share, samples)


def solution(mesh):
    return jax.shard_map(
        functools.partial(body, mesh.shape["wide"]),
        mesh=mesh,
        in_specs=(P("beam", "wide", None), P(("beam", "wide")), P(), P()),
        out_specs=P("beam", "wide", None),
        check_vma=False,
    )
```

profile of v0, /device:TPU:0, one launch (start us, length us, event | category | flops | bytes accessed | tf_op | source)
XLA Modules:
  0.0 26.5 jit_solution(6329125013609298249)
XLA Ops:
  0.0 23.8 %shard_map.109.x_ref = f32[1,16,128]{2,1,0:T(8,128)} custom-call(s32[7]{0:T(128)} %edges_ref.1, s32[16]{0:T(128)} %delays_ref.1, s32[1,256]{1,0:T(1,128)} %bitcast.4, bf16[256,4096]{1,0:T(8,128)(2,1)} %bitcast.3, f32[16,1024]{1,0:T(8,128)} %constant.14.clone.ac_ref, f32[16,1024]{1,0:T(8,128)} %constant.15.clone.as_ref, f32[32,1024]{1,0:T(8,128)} %constant.16.clone.bc_ref, ...), custom_call_target="tpu_custom_call" | custom-call | tf_op jit(solution)/shard_map/pallas_call | solution.py:356
  23.8 2.7 %shard_map.110 = f32[1,32,128]{2,1,0:T(8,128)} custom-call(f32[1,16,128]{2,1,0:T(8,128)} %shard_map.109.x_ref, f32[8,128,128]{2,1,0:T(8,128)} %constant.18.clone.fc_ref, f32[8,128,128]{2,1,0:T(8,128)} %constant.19.clone.fs_ref, f32[32,2048]{1,0:T(8,128)} %constant.20.clone.g_ref), custom_call_target="tpu_custom_call" | custom-call | tf_op jit(solution)/shard_map/pallas_call | solution.py:379
where the time goes:
time: 26.7 us; the launch traced here: 26.5 us
  Pallas kernels  26.5 us (99%)
    pallas_call x1, Pallas kernels, body(): pl.pallas_call(functools.partial(fused_kernel, n, bands, channels, trials...  23.8 us
    pallas_call x1, Pallas kernels, body(): pl.pallas_call(series_kernel, out_shape=jax.ShapeDtypeStruct((share, step...  2.74 us

commit v1 on v0

v1 whole, which is shorter than its diff:
```python
import functools
import math

import jax
import jax.numpy as jnp
import ml_dtypes
import numpy as np
from jax import lax
from jax.experimental import pallas as pl
from jax.experimental.pallas import tpu as pltpu
from jax.sharding import PartitionSpec as P

NBLK = 8
LANES = 128
VMEM = pl.BlockSpec(memory_space=pltpu.VMEM)
HBM = pl.BlockSpec(memory_space=pltpu.HBM)
MESH = pl.DeviceIdType.MESH
F32 = jnp.float32
BF16 = jnp.bfloat16


def turn_coefficients():
    degree = 5
    nodes = np.cos((np.arange(64) + 0.5) * np.pi / 64) * 0.125 + 0.125
    root = np.sqrt(nodes)
    cos_fit = np.polynomial.Chebyshev.fit(nodes, np.cos(2 * np.pi * root), degree, domain=[0, 0.25])
    sin_fit = np.polynomial.Chebyshev.fit(
        nodes, np.sin(2 * np.pi * root) / root, degree, domain=[0, 0.25]
    )
    as_power = lambda fit: [float(np.float32(v)) for v in fit.convert(kind=np.polynomial.Polynomial).coef]
    return as_power(cos_fit), as_power(sin_fit)


COS_COEF, SIN_COEF = turn_coefficients()


def cos_sin_turns(turns):
    r = turns - jnp.floor(turns + 0.5)
    s = r * r
    c = jnp.full_like(s, COS_COEF[-1])
    q = jnp.full_like(s, SIN_COEF[-1])
    for a, b in zip(COS_COEF[-2::-1], SIN_COEF[-2::-1]):
        c = c * s + a
        q = q * s + b
    return c, q * r


def forward_table(samples):
    window = samples // NBLK
    blocks = samples // 4 // 64
    r = np.arange(8)[:, None, None]
    g = 8 * np.arange(blocks)[None, :, None] + (np.arange(8)[None, None, :] ^ r)
    f = 8 * g + r
    angle = (f[..., None] * np.arange(window) % samples) * (2 * np.pi / samples)
    table = np.stack([np.cos(angle), -np.sin(angle)], axis=2)
    return table.reshape(8 * blocks * 16, window).astype(ml_dtypes.bfloat16)


def inverse_tables(samples):
    window = samples // 8
    groups = samples // 32
    g = np.arange(groups)
    t = np.arange(window)
    angle = (g[:, None] * t[None, :] % window) * (2 * np.pi / window)
    c, s = np.cos(angle), np.sin(angle)
    real = np.concatenate([c, s], axis=1).reshape(groups // 8, 8, 2 * window)
    imag = np.concatenate([-s, c], axis=1).reshape(groups // 8, 8, 2 * window)
    first = np.stack([real, imag], axis=1).reshape(2 * groups, 2 * window)
    turn = np.arange(8)[:, None] * t[None, :] * (2 * np.pi / samples)
    twist = np.concatenate([np.cos(turn), np.sin(turn)], axis=0)
    return first.astype(ml_dtypes.bfloat16), twist.astype(np.float32)


def partner(me, step, n):
    if n & (n - 1):
        return lax.rem(me + step, n)
    out, bit = 0, 1
    while bit < n:
        out = out + lax.rem(me // bit + step // bit, 2) * bit
        bit *= 2
    return out


def untangle(x):
    row = lax.broadcasted_iota(jnp.int32, x.shape, 0)
    lane = lax.broadcasted_iota(jnp.int32, x.shape, 1)
    for s in (1, 2, 4):
        low_row, low_lane = (row & s) == 0, (lane & s) == 0
        up = pltpu.roll(x, 8 - s, 0)
        right = pltpu.roll(x, s, 1)
        cross = pltpu.roll(pltpu.roll(x, LANES - s, 1), s, 0)
        x = jnp.where(low_row, jnp.where(low_lane, x, up), jnp.where(low_lane, cross, right))
    return x


def fused_kernel(
    n, bands, channels, trials,
    edges_hbm, delays_hbm, mask_hbm, x_hbm, tab_hbm, inv_hbm, twist_hbm,
    out_ref,
    edges_ref, delays_ref, mask_ref, x_ref, tab_ref, inv_ref, twist_ref, sq_ref, rot_c, rot_s, base_c, base_s,
    y_ref, spec_ref, pick_ref, scale_ref, own_power, got_power, part_ref, got_part,
    small_sem, x_sem, table_sem, power_send, power_recv, part_send, part_recv,
):
    local, samples = x_ref.shape
    window = samples // NBLK
    blocks = samples // 4 // 64
    share = out_ref.shape[0]
    gs = LANES // trials
    halves = 8 // gs
    assert gs * trials == LANES and halves * gs == 8 and 16 * blocks == 2 * LANES
    assert bands * NBLK <= LANES
    me = lax.axis_index("wide")
    first = me * local

    small = [
        pltpu.make_async_copy(src, dst, small_sem.at[i])
        for i, (src, dst) in enumerate(
            [(delays_hbm, delays_ref), (edges_hbm, edges_ref), (mask_hbm, mask_ref)]
        )
    ]
    for copy in small:
        copy.start()
    rows = 64

    def load(i):
        at = pl.ds(pl.multiple_of(i * rows, rows), rows)
        return pltpu.make_async_copy(x_hbm.at[at], x_ref.at[at], x_sem.at[i])

    for i in range(local // rows):
        load(i).start()

    barrier = pltpu.get_barrier_semaphore()
    for step in range(1, n):
        pl.semaphore_signal(
            barrier, inc=1, device_id={"wide": lax.rem(me + step, n)}, device_id_type=MESH
        )

    tables = [
        pltpu.make_async_copy(src, dst, table_sem.at[i])
        for i, (src, dst) in enumerate(
            [(tab_hbm, tab_ref), (inv_hbm, inv_ref), (twist_hbm, twist_ref)]
        )
    ]
    for copy in tables:
        copy.start()
    for copy in small:
        copy.wait()

    lane = lax.broadcasted_iota(jnp.int32, (1, LANES), 1)
    delay_row = jnp.zeros((1, LANES), F32)
    for d in range(trials):
        delay_row = jnp.where(lane // gs == d, delays_ref[d].astype(F32), delay_row)
    delay_row = delay_row * (1.0 / samples)
    offset_row = (lane % gs).astype(F32) * 8.0 + 3.5
    prow = 32

    def phases(i, carry):
        at = pl.ds(pl.multiple_of(i * prow, prow), prow)
        channel = first + i * prow + lax.broadcasted_iota(jnp.int32, (prow, LANES), 0)
        ratio = 0.5 + 0.5 * (channel.astype(F32) + 0.5) / channels
        sweep = (1.0 / (ratio * ratio) - 1.0) / 3.0 * delay_row
        half_c, half_s = cos_sin_turns(sweep * 0.5)
        twice = 4.0 * half_c * half_c - 2.0
        before, now = (half_c, -half_s), (half_c, half_s)
        for k in range(4):
            if k:
                before, now = now, tuple(twice * v - u for u, v in zip(before, now))
            rot_c[k, at, :] = now[0]
            rot_s[k, at, :] = now[1]
        step_c, step_s = cos_sin_turns(sweep * (8.0 * gs))
        a, b = cos_sin_turns(sweep * offset_row)
        old = (a * step_c + b * step_s, b * step_c - a * step_s)
        now = (a, b)
        double = step_c + step_c
        for k in range(blocks * halves):
            base_c[k, at, :] = now[0]
            base_s[k, at, :] = now[1]
            old, now = now, tuple(double * v - u for u, v in zip(old, now))
        return carry

    lax.fori_loop(0, local // prow // 2, phases, 0)

    def square(i, carry):
        load(i).wait()
        at = pl.ds(pl.multiple_of(i * rows, rows), rows)
        for k in range(NBLK):
            total = None
            for p in range(window // LANES):
                v = x_ref[at, pl.ds(k * window + p * LANES, LANES)].astype(F32)
                total = v * v if total is None else total + v * v
            sq_ref[at, pl.ds(k * LANES, LANES)] = total.astype(BF16)
        return carry

    lax.fori_loop(0, local // rows, square, 0)
    channel_row = first + lax.broadcasted_iota(jnp.int32, (1, local), 1)
    keep = mask_ref[...].astype(F32)
    picks = []
    for j in range(bands):
        inside = channel_row < (channels if j == bands - 1 else edges_ref[j])
        if j:
            inside = jnp.logical_and(inside, channel_row >= edges_ref[j - 1])
        picks.append(jnp.where(inside, keep, 0.0))
    pick = jnp.concatenate(picks, axis=0).astype(BF16)
    summed = jnp.dot(pick, sq_ref[...], preferred_element_type=F32)
    spot = lax.broadcasted_iota(jnp.int32, (bands, LANES), 1)
    band_row = lax.broadcasted_iota(jnp.int32, (bands, LANES), 0)
    powers = jnp.zeros((bands, LANES), F32)
    for k in range(NBLK):
        part = jnp.sum(summed[:, k * LANES : (k + 1) * LANES], axis=1, keepdims=True)
        powers = jnp.where(spot == band_row * NBLK + k, part, powers)
    own_power[...] = jnp.sum(powers, axis=0, keepdims=True) * (1.0 / window)

    pl.semaphore_wait(barrier, n - 1)
    power_copies = []
    for step in range(n - 1, 0, -1):
        copy = pltpu.make_async_remote_copy(
            src_ref=own_power,
            dst_ref=got_power.at[step],
            send_sem=power_send.at[step],
            recv_sem=power_recv.at[step],
            device_id={"wide": partner(me, step, n)},
            device_id_type=MESH,
        )
        copy.start()
        power_copies.append(copy)

    lax.fori_loop(local // prow // 2, local // prow, phases, 0)
    pick_ref[...] = jnp.transpose(jnp.broadcast_to(keep, (LANES, local)))
    tables[0].wait()

    total = own_power[...]
    for step in range(n - 1, 0, -1):
        power_copies[n - 1 - step].wait()
        total = total + got_power[step]
    width = jnp.zeros((1, LANES), jnp.int32)
    for j in range(bands):
        high = channels if j == bands - 1 else edges_ref[j]
        low = edges_ref[j - 1] if j else 0
        width = jnp.where(lane // NBLK == j, high - low, width)
    width = jnp.maximum(width, 1).astype(F32)
    level = 1.0 / jnp.sqrt(total / width + 1e-05)

    levels = [
        jnp.broadcast_to(pltpu.roll(level, LANES - NBLK * j, 1) if j else level, (8, LANES))
        for j in range(bands)
    ]
    for t in range(local // 8):
        at = slice(8 * t, 8 * t + 8)
        channel = first + 8 * t + lax.broadcasted_iota(jnp.int32, (8, LANES), 0)
        scale = levels[-1]
        for j in range(bands - 2, -1, -1):
            scale = jnp.where(channel < edges_ref[j], levels[j], scale)
        scale = scale * pick_ref[at, :]
        for m in range(NBLK):
            scale_ref[m, at, :] = jnp.broadcast_to(scale[:, m : m + 1], (8, LANES))

    crow = 16

    def fold(i, carry):
        at = pl.ds(pl.multiple_of(i * crow, crow), crow)
        columns = [scale_ref[m, at, :] for m in range(8)]
        root = math.sqrt(0.5)
        for p in range(window // LANES):
            here = slice(p * LANES, (p + 1) * LANES)
            x = [
                x_ref[at, m * window + p * LANES : m * window + (p + 1) * LANES].astype(F32)
                * columns[m]
                for m in range(8)
            ]
            plus = [x[m] + x[m + 4] for m in range(4)]
            minus = [x[m] - x[m + 4] for m in range(4)]
            even, odd = plus[0] + plus[2], plus[1] + plus[3]
            near, far = root * (minus[1] - minus[3]), root * (minus[1] + minus[3])
            folded = (
                even + odd, even - odd,
                minus[0] + near, -(far + minus[2]),
                plus[0] - plus[2], plus[3] - plus[1],
                minus[0] - near, minus[2] - far,
            )
            for k, value in enumerate(folded):
                y_ref[k, at, here] = value.astype(BF16)
        return carry

    lax.fori_loop(0, local // crow, fold, 0, unroll=2)

    def product(which, r):
        both = lax.dot_general(
            tab_ref[r * 16 * blocks : (r + 1) * 16 * blocks, :], y_ref[which],
            (((1,), (1,)), ((), ())), preferred_element_type=F32,
        ).reshape(blocks, 2, 8, local)
        return both[:, 0], both[:, 1]

    for r in range(8):
        if r % 4 == 0:
            re, im = product(r // 4, r)
        else:
            kind = min(r, 8 - r)
            (a_re, a_im), (b_re, b_im) = product(2 * kind, r), product(2 * kind + 1, r)
            if r < 4:
                re, im = a_re - b_im, a_im + b_re
            else:
                re, im = a_re + b_im, a_im - b_re
        spec_ref[r] = jnp.concatenate([re, im], axis=1).astype(BF16)

    row8 = lax.broadcasted_iota(jnp.int32, (8, LANES), 0)
    lane8 = lax.broadcasted_iota(jnp.int32, (8, LANES), 1) % gs
    kept = [[[] for _ in range(2)] for _ in range(halves)]
    for block in range(blocks):
        for h in range(halves):
            code = row8 ^ (lane8 + h * gs)
            xa, xb = base_c[block * halves + h], base_s[block * halves + h]
            got_re = got_im = jnp.zeros((8, LANES), F32)
            for k in range(4):
                c, s = rot_c[k], rot_s[k]
                moving = jnp.concatenate([spec_ref[3 - k, block], spec_ref[4 + k, block]], axis=0)
                one = jnp.dot(moving, jnp.concatenate([(xa * c).astype(BF16), (xb * s).astype(BF16)], axis=1), preferred_element_type=F32)
                two = jnp.dot(moving, jnp.concatenate([(xa * s).astype(BF16), (xb * c).astype(BF16)], axis=1), preferred_element_type=F32)
                ac, bs, as_, bc = one[:, :LANES], one[:, LANES:], two[:, :LANES], two[:, LANES:]
                re, im = slice(0, 8), slice(8, 16)
                out_re = (ac[re] + bs[re]) - (bc[im] - as_[im])
                out_im = (bc[re] - as_[re]) + (ac[im] + bs[im])
                got_re = jnp.where(code == 3 - k, out_re, got_re)
                got_im = jnp.where(code == 3 - k, out_im, got_im)
                re, im = slice(16, 24), slice(24, 32)
                out_re = (ac[re] - bs[re]) - (as_[im] + bc[im])
                out_im = (as_[re] + bc[re]) + (ac[im] - bs[im])
                got_re = jnp.where(code == 4 + k, out_re, got_re)
                got_im = jnp.where(code == 4 + k, out_im, got_im)
            kept[h][2 * block // blocks].append(jnp.concatenate([got_re, got_im], axis=0))
    turned = [[jnp.transpose(jnp.concatenate(v, axis=0)) for v in pair] for pair in kept]
    for d in range(trials):
        at = slice(d * gs, (d + 1) * gs)
        pieces = [turned[h][side][at] for side in range(2) for h in range(halves)]
        part_ref[d] = jnp.concatenate(pieces, axis=0).astype(BF16)

    def part_copy(step):
        to = partner(me, step, n)
        return pltpu.make_async_remote_copy(
            src_ref=part_ref.at[pl.ds(to * share, share)],
            dst_ref=got_part.at[step],
            send_sem=part_send.at[step],
            recv_sem=part_recv.at[step],
            device_id={"wide": to},
            device_id_type=MESH,
        )

    for step in range(n - 1, 0, -1):
        part_copy(step).start()
    for copy in tables[1:]:
        copy.wait()
    totals = [part_ref[me * share + sub].astype(F32) for sub in range(share)]
    for step in range(n - 1, 0, -1):
        part_copy(step).wait()
        totals = [t + got_part[step, sub].astype(F32) for sub, t in enumerate(totals)]

    col = lax.broadcasted_iota(jnp.int32, (8, LANES), 1)
    t_c, t_s = cos_sin_turns(((col % 8) * row8).astype(F32) * 0.125)
    mix = jnp.where(col % 16 < 8, t_c, -t_s)[:, :32].astype(BF16)
    for sub in range(share):
        lower, upper = untangle(totals[sub][:8]), untangle(totals[sub][8:])
        zero_bin = jnp.logical_and(row8 == 0, jnp.logical_or(col == 0, col == 8))
        lower = jnp.where(zero_bin, 0.5 * lower, lower)
        bins = jnp.concatenate([lower, upper], axis=1).astype(BF16)
        a = jnp.dot(bins, inv_ref[...], preferred_element_type=F32)
        a_re, a_im = a[:, :window], a[:, window:]
        w_re, w_im = twist_ref[0:8, :], twist_ref[8:16, :]
        b = jnp.concatenate([a_re * w_re - a_im * w_im, a_re * w_im + a_im * w_re], axis=0)
        high = b.astype(BF16)
        low = (b - high.astype(F32)).astype(BF16)
        out = jnp.dot(mix, jnp.concatenate([high, low], axis=0), preferred_element_type=F32)
        out = out * (2.0 / (samples * math.sqrt(channels)))
        per = window // LANES
        for p in range(per):
            out_ref[sub, pl.ds(p, 8, stride=per), :] = out[:, p * LANES : (p + 1) * LANES]


def body(n, filterbank, channel_mask, band_edges, dm_delays):
    beams, local, samples = filterbank.shape
    channels = local * n
    bands = band_edges.shape[0] + 1
    trials = dm_delays.shape[0]
    share = trials // n
    window = samples // NBLK
    blocks = samples // 4 // 64
    halves = 8 // (LANES // trials)
    tab = forward_table(samples)
    inv, twist = inverse_tables(samples)
    x = filterbank.reshape(local, samples)

    dma = pltpu.SemaphoreType.DMA((n,))
    series = pl.pallas_call(
        functools.partial(fused_kernel, n, bands, channels, trials),
        out_shape=jax.ShapeDtypeStruct((share, samples // LANES, LANES), F32),
        in_specs=[HBM] * 7,
        out_specs=VMEM,
        scratch_shapes=[
            pltpu.SMEM(band_edges.shape, jnp.int32),
            pltpu.SMEM(dm_delays.shape, jnp.int32),
            pltpu.VMEM((1, local), jnp.int32),
            pltpu.VMEM((local, samples), x.dtype),
            pltpu.VMEM(tab.shape, BF16),
            pltpu.VMEM(inv.shape, BF16),
            pltpu.VMEM(twist.shape, F32),
            pltpu.VMEM((local, NBLK * LANES), BF16),
            pltpu.VMEM((4, local, LANES), F32),
            pltpu.VMEM((4, local, LANES), F32),
            pltpu.VMEM((blocks * halves, local, LANES), F32),
            pltpu.VMEM((blocks * halves, local, LANES), F32),
            pltpu.VMEM((8, local, window), BF16),
            pltpu.VMEM((8, blocks, 16, local), BF16),
            pltpu.VMEM((local, LANES), F32),
            pltpu.VMEM((NBLK, local, LANES), F32),
            pltpu.VMEM((1, LANES), F32),
            pltpu.VMEM((n, 1, LANES), F32),
            pltpu.VMEM((trials, 16, LANES), BF16),
            pltpu.VMEM((n, share, 16, LANES), BF16),
            pltpu.SemaphoreType.DMA((3,)), pltpu.SemaphoreType.DMA((local // 64,)), pltpu.SemaphoreType.DMA((3,)),
            dma, dma, dma, dma,
        ],
        compiler_params=pltpu.CompilerParams(
            collective_id=0, has_side_effects=True, vmem_limit_bytes=24 << 20
        ),
    )(*[
        pltpu.with_memory_space_constraint(v, pltpu.HBM)
        for v in (
            band_edges, dm_delays, channel_mask.reshape(1, local), x,
            jnp.asarray(tab), jnp.asarray(inv), jnp.asarray(twist),
        )
    ])
    return series.reshape(beams, share, samples)


def solution(mesh):
    return jax.shard_map(
        functools.partial(body, mesh.shape["wide"]),
        mesh=mesh,
        in_specs=(P("beam", "wide", None), P(("beam", "wide")), P(), P()),
        out_specs=P("beam", "wide", None),
        check_vma=False,
    )
```

time: 26.7 us -> 21.5 us (0.81)
  Pallas kernels: 26.5 us -> 20.8 us
  local copies, waits for them, and re-layouts: 0 us -> 0.61 us
    pallas_call x1, Pallas kernels: 23.8 us -> 20.8 us  [body(): pl.pallas_call(functools.partial(fused_kernel, n, bands, channels, trials...]
    pallas_call x1 -> x0, Pallas kernels: 2.74 us -> none  [body(): pl.pallas_call(series_kernel, out_shape=jax.ShapeDtypeStruct((share, step...]
    unnamed x0 -> x1, local copies, waits for them, and re-layouts: none -> 0.61 us
where the time goes in v1:
time: 21.5 us; the launch traced here: 21.4 us
  Pallas kernels  20.8 us (97%)
  local copies, waits for them, and re-layouts  0.61 us (3%)
    pallas_call x1, Pallas kernels, body(): pl.pallas_call(functools.partial(fused_kernel, n, bands, channels, trials...  20.8 us
    unnamed x1, local copies, waits for them, and re-layouts  0.61 us

profile of v1, /device:TPU:0, one launch (start us, length us, event | category | flops | bytes accessed | tf_op | source)
XLA Modules:
  0.0 21.4 jit_solution(10194319655403052844)
XLA Ops:
  0.0 20.8 %shard_map.73 = f32[1,32,128]{2,1,0:T(8,128)S(1)} custom-call(s32[7]{0:T(128)} %edges_hbm.1, s32[16]{0:T(128)} %delays_hbm.1, s32[1,256]{1,0:T(1,128)} %bitcast.5, bf16[256,4096]{1,0:T(8,128)(2,1)} %bitcast.4, bf16[2048,512]{1,0:T(8,128)(2,1)} %constant.6.clone.tab_hbm, bf16[256,1024]{1,0:T(8,128)(2,1)} %constant.7.clone.inv_hbm, ...), custom_call_target="tpu_custom_call" | custom-call | tf_op jit(solution)/shard_map/pallas_call | solution.py:391
  20.8 0.6 %copy.9 = f32[1,1,4096]{2,1,0:T(1,128)} copy(f32[1,1,4096]{2,1,0:T(1,128)S(1)} %bitcast.3) | data formatting | bytes 32768

commit v2 on v1

--- a/solution.py
+++ b/solution.py
@@ -12,6 +12,7 @@
 
 NBLK = 8
 LANES = 128
+PARTS = 4
 VMEM = pl.BlockSpec(memory_space=pltpu.VMEM)
 HBM = pl.BlockSpec(memory_space=pltpu.HBM)
 MESH = pl.DeviceIdType.MESH
@@ -56,10 +57,11 @@
     return table.reshape(8 * blocks * 16, window).astype(ml_dtypes.bfloat16)
 
 
-def inverse_tables(samples):
+def inverse_tables(samples, gs):
     window = samples // 8
     groups = samples // 32
-    g = np.arange(groups)
+    row, high, part, low = np.ix_(range(2), range(gs // 16), range(groups // gs), range(8))
+    g = (gs * part + 8 * (2 * high + row) + low).reshape(-1)
     t = np.arange(window)
     angle = (g[:, None] * t[None, :] % window) * (2 * np.pi / window)
     c, s = np.cos(angle), np.sin(angle)
@@ -69,16 +71,6 @@
     turn = np.arange(8)[:, None] * t[None, :] * (2 * np.pi / samples)
     twist = np.concatenate([np.cos(turn), np.sin(turn)], axis=0)
     return first.astype(ml_dtypes.bfloat16), twist.astype(np.float32)
-
-
-def partner(me, step, n):
-    if n & (n - 1):
-        return lax.rem(me + step, n)
-    out, bit = 0, 1
-    while bit < n:
-        out = out + lax.rem(me // bit + step // bit, 2) * bit
-        bit *= 2
-    return out
 
 
 def untangle(x):
@@ -98,19 +90,38 @@
     edges_hbm, delays_hbm, mask_hbm, x_hbm, tab_hbm, inv_hbm, twist_hbm,
     out_ref,
     edges_ref, delays_ref, mask_ref, x_ref, tab_ref, inv_ref, twist_ref, sq_ref, rot_c, rot_s, base_c, base_s,
-    y_ref, spec_ref, pick_ref, scale_ref, own_power, got_power, part_ref, got_part,
+    y_ref, spec_ref, pick_ref, own_power, got_power, part_ref, got_part,
     small_sem, x_sem, table_sem, power_send, power_recv, part_send, part_recv,
 ):
     local, samples = x_ref.shape
     window = samples // NBLK
     blocks = samples // 4 // 64
     share = out_ref.shape[0]
-    gs = LANES // trials
-    halves = 8 // gs
-    assert gs * trials == LANES and halves * gs == 8 and 16 * blocks == 2 * LANES
+    some = trials // PARTS
+    gs = LANES // some
+    supers = 8 * blocks // gs
+    near = gs // 8
+    assert gs * some == LANES and gs in (16, 32) and 8 * blocks == LANES
+    assert n & (n - 1) == 0 and n * share == trials
     assert bands * NBLK <= LANES
     me = lax.axis_index("wide")
     first = me * local
+
+    def wait_all(slots, sem):
+        others = slots.at[pl.ds(1, n - 1)]
+        pltpu.make_async_copy(others, others, sem).wait()
+
+    flips = []
+    while 1 << len(flips) < n:
+        bit = 1 << len(flips)
+        flips.append(bit - 2 * bit * lax.rem(me // bit, 2))
+
+    def partner(step):
+        to = me
+        for b, flip in enumerate(flips):
+            if step >> b & 1:
+                to = to + flip
+        return to
 
     small = [
         pltpu.make_async_copy(src, dst, small_sem.at[i])
@@ -130,10 +141,8 @@
         load(i).start()
 
     barrier = pltpu.get_barrier_semaphore()
-    for step in range(1, n):
-        pl.semaphore_signal(
-            barrier, inc=1, device_id={"wide": lax.rem(me + step, n)}, device_id_type=MESH
-        )
+    for step in range(n - 1, 0, -1):
+        pl.semaphore_signal(barrier, inc=1, device_id={"wide": partner(step)}, device_id_type=MESH)
 
     tables = [
         pltpu.make_async_copy(src, dst, table_sem.at[i])
@@ -147,10 +156,12 @@
         copy.wait()
 
     lane = lax.broadcasted_iota(jnp.int32, (1, LANES), 1)
-    delay_row = jnp.zeros((1, LANES), F32)
-    for d in range(trials):
-        delay_row = jnp.where(lane // gs == d, delays_ref[d].astype(F32), delay_row)
-    delay_row = delay_row * (1.0 / samples)
+    delay_rows = []
+    for side in range(PARTS):
+        row = jnp.zeros((1, LANES), F32)
+        for d in range(some):
+            row = jnp.where(lane // gs == d, delays_ref[side * some + d].astype(F32), row)
+        delay_rows.append(row * (1.0 / samples))
     offset_row = (lane % gs).astype(F32) * 8.0 + 3.5
     prow = 32
 
@@ -158,27 +169,27 @@
         at = pl.ds(pl.multiple_of(i * prow, prow), prow)
         channel = first + i * prow + lax.broadcasted_iota(jnp.int32, (prow, LANES), 0)
         ratio = 0.5 + 0.5 * (channel.astype(F32) + 0.5) / channels
-        sweep = (1.0 / (ratio * ratio) - 1.0) / 3.0 * delay_row
-        half_c, half_s = cos_sin_turns(sweep * 0.5)
-        twice = 4.0 * half_c * half_c - 2.0
-        before, now = (half_c, -half_s), (half_c, half_s)
-        for k in range(4):
-            if k:
-                before, now = now, tuple(twice * v - u for u, v in zip(before, now))
-            rot_c[k, at, :] = now[0]
-            rot_s[k, at, :] = now[1]
-        step_c, step_s = cos_sin_turns(sweep * (8.0 * gs))
-        a, b = cos_sin_turns(sweep * offset_row)
-        old = (a * step_c + b * step_s, b * step_c - a * step_s)
-        now = (a, b)
-        double = step_c + step_c
-        for k in range(blocks * halves):
-            base_c[k, at, :] = now[0]
-            base_s[k, at, :] = now[1]
-            old, now = now, tuple(double * v - u for u, v in zip(old, now))
+        fraction = (1.0 / (ratio * ratio) - 1.0) / 3.0
+        for side, delay_row in enumerate(delay_rows):
+            sweep = fraction * delay_row
+            half_c, half_s = cos_sin_turns(sweep * 0.5)
+            twice = 4.0 * half_c * half_c - 2.0
+            before, now = (half_c, -half_s), (half_c, half_s)
+            for k in range(4):
+                if k:
+                    before, now = now, tuple(twice * v - u for u, v in zip(before, now))
+                rot_c[4 * side + k, at, :] = now[0]
+                rot_s[4 * side + k, at, :] = now[1]
+            step_c, step_s = cos_sin_turns(sweep * (8.0 * gs))
+            a, b = cos_sin_turns(sweep * offset_row)
+            old = (a * step_c + b * step_s, b * step_c - a * step_s)
+            now = (a, b)
+            double = step_c + step_c
+            for k in range(supers):
+                base_c[side * supers + k, at, :] = now[0].astype(BF16)
+                base_s[side * supers + k, at, :] = now[1].astype(BF16)
+                old, now = now, tuple(double * v - u for u, v in zip(old, now))
         return carry
-
-    lax.fori_loop(0, local // prow // 2, phases, 0)
 
     def square(i, carry):
         load(i).wait()
@@ -211,26 +222,23 @@
     own_power[...] = jnp.sum(powers, axis=0, keepdims=True) * (1.0 / window)
 
     pl.semaphore_wait(barrier, n - 1)
-    power_copies = []
     for step in range(n - 1, 0, -1):
-        copy = pltpu.make_async_remote_copy(
+        pltpu.make_async_remote_copy(
             src_ref=own_power,
             dst_ref=got_power.at[step],
-            send_sem=power_send.at[step],
-            recv_sem=power_recv.at[step],
-            device_id={"wide": partner(me, step, n)},
+            send_sem=power_send,
+            recv_sem=power_recv,
+            device_id={"wide": partner(step)},
             device_id_type=MESH,
-        )
-        copy.start()
-        power_copies.append(copy)
-
-    lax.fori_loop(local // prow // 2, local // prow, phases, 0)
+        ).start()
+
+    lax.fori_loop(0, local // prow, phases, 0)
     pick_ref[...] = jnp.transpose(jnp.broadcast_to(keep, (LANES, local)))
     tables[0].wait()
 
     total = own_power[...]
+    wait_all(got_power, power_recv)
     for step in range(n - 1, 0, -1):
-        power_copies[n - 1 - step].wait()
         total = total + got_power[step]
     width = jnp.zeros((1, LANES), jnp.int32)
     for j in range(bands):
@@ -250,15 +258,13 @@
         scale = levels[-1]
         for j in range(bands - 2, -1, -1):
             scale = jnp.where(channel < edges_ref[j], levels[j], scale)
-        scale = scale * pick_ref[at, :]
-        for m in range(NBLK):
-            scale_ref[m, at, :] = jnp.broadcast_to(scale[:, m : m + 1], (8, LANES))
-
+        pick_ref[at, :] = scale * pick_ref[at, :]
     crow = 16
 
     def fold(i, carry):
         at = pl.ds(pl.multiple_of(i * crow, crow), crow)
-        columns = [scale_ref[m, at, :] for m in range(8)]
+        scale = pick_ref[at, :]
+        columns = [jnp.broadcast_to(scale[:, m : m + 1], (crow, LANES)) for m in range(8)]
         root = math.sqrt(0.5)
         for p in range(window // LANES):
             here = slice(p * LANES, (p + 1) * LANES)
@@ -281,7 +287,7 @@
                 y_ref[k, at, here] = value.astype(BF16)
         return carry
 
-    lax.fori_loop(0, local // crow, fold, 0, unroll=2)
+    lax.fori_loop(0, local // crow, fold, 0, unroll=True)
 
     def product(which, r):
         both = lax.dot_general(
@@ -304,58 +310,77 @@
 
     row8 = lax.broadcasted_iota(jnp.int32, (8, LANES), 0)
     lane8 = lax.broadcasted_iota(jnp.int32, (8, LANES), 1) % gs
-    kept = [[[] for _ in range(2)] for _ in range(halves)]
-    for block in range(blocks):
-        for h in range(halves):
-            code = row8 ^ (lane8 + h * gs)
-            xa, xb = base_c[block * halves + h], base_s[block * halves + h]
-            got_re = got_im = jnp.zeros((8, LANES), F32)
-            for k in range(4):
-                c, s = rot_c[k], rot_s[k]
-                moving = jnp.concatenate([spec_ref[3 - k, block], spec_ref[4 + k, block]], axis=0)
-                one = jnp.dot(moving, jnp.concatenate([(xa * c).astype(BF16), (xb * s).astype(BF16)], axis=1), preferred_element_type=F32)
-                two = jnp.dot(moving, jnp.concatenate([(xa * s).astype(BF16), (xb * c).astype(BF16)], axis=1), preferred_element_type=F32)
-                ac, bs, as_, bc = one[:, :LANES], one[:, LANES:], two[:, :LANES], two[:, LANES:]
-                re, im = slice(0, 8), slice(8, 16)
-                out_re = (ac[re] + bs[re]) - (bc[im] - as_[im])
-                out_im = (bc[re] - as_[re]) + (ac[im] + bs[im])
-                got_re = jnp.where(code == 3 - k, out_re, got_re)
-                got_im = jnp.where(code == 3 - k, out_im, got_im)
-                re, im = slice(16, 24), slice(24, 32)
-                out_re = (ac[re] - bs[re]) - (as_[im] + bc[im])
-                out_im = (as_[re] + bc[re]) + (ac[im] - bs[im])
-                got_re = jnp.where(code == 4 + k, out_re, got_re)
-                got_im = jnp.where(code == 4 + k, out_im, got_im)
-            kept[h][2 * block // blocks].append(jnp.concatenate([got_re, got_im], axis=0))
-    turned = [[jnp.transpose(jnp.concatenate(v, axis=0)) for v in pair] for pair in kept]
-    for d in range(trials):
-        at = slice(d * gs, (d + 1) * gs)
-        pieces = [turned[h][side][at] for side in range(2) for h in range(halves)]
-        part_ref[d] = jnp.concatenate(pieces, axis=0).astype(BF16)
-
-    def part_copy(step):
-        to = partner(me, step, n)
+    code = (row8 ^ (lane8 % 8)) + lane8 // 8 * 8
+    fourth = n // PARTS
+    corner = lax.rem(me, fourth)
+    bits = [lax.rem(me // (fourth << b), 2) for b in range(PARTS.bit_length() - 1)]
+
+    def part_copy(step, to):
         return pltpu.make_async_remote_copy(
             src_ref=part_ref.at[pl.ds(to * share, share)],
             dst_ref=got_part.at[step],
-            send_sem=part_send.at[step],
-            recv_sem=part_recv.at[step],
+            send_sem=part_send,
+            recv_sem=part_recv,
             device_id={"wide": to},
             device_id_type=MESH,
         )
 
-    for step in range(n - 1, 0, -1):
-        part_copy(step).start()
+    for side in range(PARTS):
+        kept = []
+        for block in range(supers):
+            xa, xb = base_c[side * supers + block], base_s[side * supers + block]
+            got_re = got_im = jnp.zeros((8, LANES), F32)
+            for k in range(4):
+                c, s = rot_c[4 * side + k].astype(BF16), rot_s[4 * side + k].astype(BF16)
+                moving = jnp.concatenate(
+                    [spec_ref[j, near * block + q] for j in (3 - k, 4 + k) for q in range(near)], axis=0
+                )
+                one = jnp.concatenate([c * xa, s * xb], axis=1)
+                two = jnp.concatenate([s * xa, c * xb], axis=1)
+                one = jnp.dot(moving, one, preferred_element_type=F32)
+                two = jnp.dot(moving, two, preferred_element_type=F32)
+                ac, bs, as_, bc = one[:, :LANES], one[:, LANES:], two[:, :LANES], two[:, LANES:]
+                for q in range(near):
+                    re = slice(16 * q, 16 * q + 8)
+                    im = slice(16 * q + 8, 16 * q + 16)
+                    out_re = (ac[re] + bs[re]) - (bc[im] - as_[im])
+                    out_im = (bc[re] - as_[re]) + (ac[im] + bs[im])
+                    got_re = jnp.where(code == 8 * q + 3 - k, out_re, got_re)
+                    got_im = jnp.where(code == 8 * q + 3 - k, out_im, got_im)
+                    re = slice(16 * (near + q), 16 * (near + q) + 8)
+                    im = slice(16 * (near + q) + 8, 16 * (near + q) + 16)
+                    out_re = (ac[re] - bs[re]) - (as_[im] + bc[im])
+                    out_im = (as_[re] + bc[re]) + (ac[im] - bs[im])
+                    got_re = jnp.where(code == 8 * q + 4 + k, out_re, got_re)
+                    got_im = jnp.where(code == 8 * q + 4 + k, out_im, got_im)
+            kept.append(jnp.concatenate([got_re, got_im], axis=0))
+        turned = jnp.transpose(jnp.concatenate(kept, axis=0))
+        for d in range(some):
+            pieces = [turned[u : u + 16] for u in range(d * gs, (d + 1) * gs, 16)]
+            part_ref[side * some + d] = jnp.concatenate(pieces, axis=1).astype(BF16)
+        flipped = [1 - v if side >> b & 1 else v for b, v in enumerate(bits)]
+        base = sum(v * (fourth << b) for b, v in enumerate(flipped))
+        for i in range(fourth - 1, 0, -1):
+            to = side * fourth + corner
+            for b, flip in enumerate(flips):
+                if i >> b & 1:
+                    to = to + flip
+            part_copy(base + i, to).start()
+
+        @pl.when(base > 0)
+        def _():
+            part_copy(base, side * fourth + corner).start()
+
+    col = lax.broadcasted_iota(jnp.int32, (8, LANES), 1)
+    t_c, t_s = cos_sin_turns(((col % 8) * row8).astype(F32) * 0.125)
+    mix = jnp.where(col % 16 < 8, t_c, -t_s)[:, :32].astype(BF16)
     for copy in tables[1:]:
         copy.wait()
     totals = [part_ref[me * share + sub].astype(F32) for sub in range(share)]
+    wait_all(got_part, part_recv)
     for step in range(n - 1, 0, -1):
-        part_copy(step).wait()
         totals = [t + got_part[step, sub].astype(F32) for sub, t in enumerate(totals)]
 
-    col = lax.broadcasted_iota(jnp.int32, (8, LANES), 1)
-    t_c, t_s = cos_sin_turns(((col % 8) * row8).astype(F32) * 0.125)
-    mix = jnp.where(col % 16 < 8, t_c, -t_s)[:, :32].astype(BF16)
     for sub in range(share):
         lower, upper = untangle(totals[sub][:8]), untangle(totals[sub][8:])
         zero_bin = jnp.logical_and(row8 == 0, jnp.logical_or(col == 0, col == 8))
@@ -372,6 +397,8 @@
         per = window // LANES
         for p in range(per):
             out_ref[sub, pl.ds(p, 8, stride=per), :] = out[:, p * LANES : (p + 1) * LANES]
+    wait_all(got_power, power_send)
+    wait_all(got_part, part_send)
 
 
 def body(n, filterbank, channel_mask, band_edges, dm_delays):
@@ -381,13 +408,13 @@
     trials = dm_delays.shape[0]
     share = trials // n
     window = samples // NBLK
-    blocks = samples // 4 // 64
-    halves = 8 // (LANES // trials)
+    gs = PARTS * LANES // trials
+    supers = samples // 32 // gs
     tab = forward_table(samples)
-    inv, twist = inverse_tables(samples)
+    inv, twist = inverse_tables(samples, gs)
     x = filterbank.reshape(local, samples)
 
-    dma = pltpu.SemaphoreType.DMA((n,))
+    dma = pltpu.SemaphoreType.DMA
     series = pl.pallas_call(
         functools.partial(fused_kernel, n, bands, channels, trials),
         out_shape=jax.ShapeDtypeStruct((share, samples // LANES, LANES), F32),
@@ -402,14 +429,13 @@
             pltpu.VMEM(inv.shape, BF16),
             pltpu.VMEM(twist.shape, F32),
             pltpu.VMEM((local, NBLK * LANES), BF16),
-            pltpu.VMEM((4, local, LANES), F32),
-            pltpu.VMEM((4, local, LANES), F32),
-            pltpu.VMEM((blocks * halves, local, LANES), F32),
-            pltpu.VMEM((blocks * halves, local, LANES), F32),
+            pltpu.VMEM((4 * PARTS, local, LANES), F32),
+            pltpu.VMEM((4 * PARTS, local, LANES), F32),
+            pltpu.VMEM((PARTS * supers, local, LANES), BF16),
+            pltpu.VMEM((PARTS * supers, local, LANES), BF16),
             pltpu.VMEM((8, local, window), BF16),
-            pltpu.VMEM((8, blocks, 16, local), BF16),
+            pltpu.VMEM((8, samples // 256, 16, local), BF16),
             pltpu.VMEM((local, LANES), F32),
-            pltpu.VMEM((NBLK, local, LANES), F32),
             pltpu.VMEM((1, LANES), F32),
             pltpu.VMEM((n, 1, LANES), F32),
             pltpu.VMEM((trials, 16, LANES), BF16),

time: 21.5 us -> 18.3 us (0.85)
  Pallas kernels: 20.8 us -> 17.5 us
    pallas_call x1, Pallas kernels: 20.8 us -> 17.5 us  [body(): pl.pallas_call(functools.partial(fused_kernel, n, bands, channels, trials...]
where the time goes in v2:
time: 18.3 us; the launch traced here: 18.1 us
  Pallas kernels  17.5 us (96%)
  local copies, waits for them, and re-layouts  0.61 us (3%)
    pallas_call x1, Pallas kernels, body(): pl.pallas_call(functools.partial(fused_kernel, n, bands, channels, trials...  17.5 us
    unnamed x1, local copies, waits for them, and re-layouts  0.61 us

profile of v2, /device:TPU:0, one launch (start us, length us, event | category | flops | bytes accessed | tf_op | source)
XLA Modules:
  0.0 18.1 jit_solution(12611502467593852769)
XLA Ops:
  0.0 17.5 %shard_map.73 = f32[1,32,128]{2,1,0:T(8,128)S(1)} custom-call(s32[7]{0:T(128)} %edges_hbm.1, s32[16]{0:T(128)} %delays_hbm.1, s32[1,256]{1,0:T(1,128)} %bitcast.5, bf16[256,4096]{1,0:T(8,128)(2,1)} %bitcast.4, bf16[2048,512]{1,0:T(8,128)(2,1)} %constant.6.clone.tab_hbm, bf16[256,1024]{1,0:T(8,128)(2,1)} %constant.7.clone.inv_hbm, ...), custom_call_target="tpu_custom_call" | custom-call | tf_op jit(solution)/shard_map/pallas_call | solution.py:418
  17.5 0.6 %copy.9 = f32[1,1,4096]{2,1,0:T(1,128)} copy(f32[1,1,4096]{2,1,0:T(1,128)S(1)} %bitcast.3) | data formatting | bytes 32768

commit v3 on v2

--- a/solution.py
+++ b/solution.py
@@ -13,6 +13,7 @@
 NBLK = 8
 LANES = 128
 PARTS = 4
+ORDER = (0, 4, 1, 7, 2, 6, 3, 5)
 VMEM = pl.BlockSpec(memory_space=pltpu.VMEM)
 HBM = pl.BlockSpec(memory_space=pltpu.HBM)
 MESH = pl.DeviceIdType.MESH
@@ -49,7 +50,7 @@
 def forward_table(samples):
     window = samples // NBLK
     blocks = samples // 4 // 64
-    r = np.arange(8)[:, None, None]
+    r = np.array(ORDER)[:, None, None]
     g = 8 * np.arange(blocks)[None, :, None] + (np.arange(8)[None, None, :] ^ r)
     f = 8 * g + r
     angle = (f[..., None] * np.arange(window) % samples) * (2 * np.pi / samples)
@@ -90,8 +91,8 @@
     edges_hbm, delays_hbm, mask_hbm, x_hbm, tab_hbm, inv_hbm, twist_hbm,
     out_ref,
     edges_ref, delays_ref, mask_ref, x_ref, tab_ref, inv_ref, twist_ref, sq_ref, rot_c, rot_s, base_c, base_s,
-    y_ref, spec_ref, pick_ref, own_power, got_power, part_ref, got_part,
-    small_sem, x_sem, table_sem, power_send, power_recv, part_send, part_recv,
+    y_ref, minus_ref, spec_ref, pick_ref, own_power, got_power, part_ref, got_part,
+    small_sem, x_sem, send_sem, power_recv, part_recv,
 ):
     local, samples = x_ref.shape
     window = samples // NBLK
@@ -133,27 +134,23 @@
         copy.start()
     rows = 64
 
-    def load(i):
-        at = pl.ds(pl.multiple_of(i * rows, rows), rows)
-        return pltpu.make_async_copy(x_hbm.at[at], x_ref.at[at], x_sem.at[i])
-
-    for i in range(local // rows):
-        load(i).start()
+    whole = pltpu.make_async_copy(x_hbm, x_ref, x_sem)
+    whole.start()
 
     barrier = pltpu.get_barrier_semaphore()
     for step in range(n - 1, 0, -1):
         pl.semaphore_signal(barrier, inc=1, device_id={"wide": partner(step)}, device_id_type=MESH)
 
     tables = [
-        pltpu.make_async_copy(src, dst, table_sem.at[i])
+        pltpu.make_async_copy(src, dst, small_sem.at[i])
         for i, (src, dst) in enumerate(
             [(tab_hbm, tab_ref), (inv_hbm, inv_ref), (twist_hbm, twist_ref)]
         )
     ]
+    for copy in small:
+        copy.wait()
     for copy in tables:
         copy.start()
-    for copy in small:
-        copy.wait()
 
     lane = lax.broadcasted_iota(jnp.int32, (1, LANES), 1)
     delay_rows = []
@@ -192,7 +189,6 @@
         return carry
 
     def square(i, carry):
-        load(i).wait()
         at = pl.ds(pl.multiple_of(i * rows, rows), rows)
         for k in range(NBLK):
             total = None
@@ -202,6 +198,7 @@
             sq_ref[at, pl.ds(k * LANES, LANES)] = total.astype(BF16)
         return carry
 
+    whole.wait()
     lax.fori_loop(0, local // rows, square, 0)
     channel_row = first + lax.broadcasted_iota(jnp.int32, (1, local), 1)
     keep = mask_ref[...].astype(F32)
@@ -226,7 +223,7 @@
         pltpu.make_async_remote_copy(
             src_ref=own_power,
             dst_ref=got_power.at[step],
-            send_sem=power_send,
+            send_sem=send_sem,
             recv_sem=power_recv,
             device_id={"wide": partner(step)},
             device_id_type=MESH,
@@ -237,6 +234,7 @@
     tables[0].wait()
 
     total = own_power[...]
+    wait_all(got_power, send_sem)
     wait_all(got_power, power_recv)
     for step in range(n - 1, 0, -1):
         total = total + got_power[step]
@@ -261,11 +259,9 @@
         pick_ref[at, :] = scale * pick_ref[at, :]
     crow = 16
 
-    def fold(i, carry):
-        at = pl.ds(pl.multiple_of(i * crow, crow), crow)
+    def fold(at):
         scale = pick_ref[at, :]
         columns = [jnp.broadcast_to(scale[:, m : m + 1], (crow, LANES)) for m in range(8)]
-        root = math.sqrt(0.5)
         for p in range(window // LANES):
             here = slice(p * LANES, (p + 1) * LANES)
             x = [
@@ -276,50 +272,65 @@
             plus = [x[m] + x[m + 4] for m in range(4)]
             minus = [x[m] - x[m + 4] for m in range(4)]
             even, odd = plus[0] + plus[2], plus[1] + plus[3]
+            folded = (
+                (0, even + odd), (1, even - odd), (4, plus[0] - plus[2]), (5, plus[3] - plus[1]),
+            )
+            for k, value in folded:
+                y_ref[k, at, here] = value.astype(BF16)
+            for k in range(4):
+                minus_ref[k, at, here] = minus[k]
+
+    for i in range(local // crow):
+        fold(slice(i * crow, (i + 1) * crow))
+
+    def fold_rest(at):
+        root = math.sqrt(0.5)
+        for p in range(window // LANES):
+            here = slice(p * LANES, (p + 1) * LANES)
+            minus = [minus_ref[k, at, here] for k in range(4)]
             near, far = root * (minus[1] - minus[3]), root * (minus[1] + minus[3])
             folded = (
-                even + odd, even - odd,
-                minus[0] + near, -(far + minus[2]),
-                plus[0] - plus[2], plus[3] - plus[1],
-                minus[0] - near, minus[2] - far,
+                (2, minus[0] + near), (3, -(far + minus[2])),
+                (6, minus[0] - near), (7, minus[2] - far),
             )
-            for k, value in enumerate(folded):
+            for k, value in folded:
                 y_ref[k, at, here] = value.astype(BF16)
-        return carry
-
-    lax.fori_loop(0, local // crow, fold, 0, unroll=True)
-
-    def product(which, r):
+
+
+    def product(which, first_row, count):
+        size = 16 * blocks
         both = lax.dot_general(
-            tab_ref[r * 16 * blocks : (r + 1) * 16 * blocks, :], y_ref[which],
+            tab_ref[first_row * size : (first_row + count) * size, :], y_ref[which],
             (((1,), (1,)), ((), ())), preferred_element_type=F32,
-        ).reshape(blocks, 2, 8, local)
-        return both[:, 0], both[:, 1]
-
-    for r in range(8):
-        if r % 4 == 0:
-            re, im = product(r // 4, r)
-        else:
-            kind = min(r, 8 - r)
-            (a_re, a_im), (b_re, b_im) = product(2 * kind, r), product(2 * kind + 1, r)
-            if r < 4:
-                re, im = a_re - b_im, a_im + b_re
-            else:
-                re, im = a_re + b_im, a_im - b_re
+        ).reshape(count, blocks, 2, 8, local)
+        return both[:, :, 0], both[:, :, 1]
+
+    def keep_spectrum(r, re, im):
         spec_ref[r] = jnp.concatenate([re, im], axis=1).astype(BF16)
+
+    for which in range(2):
+        re, im = product(which, which, 1)
+        keep_spectrum(ORDER[which], re[0], im[0])
+    for kind in (2, 1, 3):
+        if kind == 1:
+            for i in range(local // crow):
+                fold_rest(slice(i * crow, (i + 1) * crow))
+        (a_re, a_im), (b_re, b_im) = product(2 * kind, 2 * kind, 2), product(2 * kind + 1, 2 * kind, 2)
+        keep_spectrum(kind, a_re[0] - b_im[0], a_im[0] + b_re[0])
+        keep_spectrum(8 - kind, a_re[1] + b_im[1], a_im[1] - b_re[1])
 
     row8 = lax.broadcasted_iota(jnp.int32, (8, LANES), 0)
     lane8 = lax.broadcasted_iota(jnp.int32, (8, LANES), 1) % gs
     code = (row8 ^ (lane8 % 8)) + lane8 // 8 * 8
     fourth = n // PARTS
-    corner = lax.rem(me, fourth)
+    low_bits = [lax.rem(me // (1 << b), 2) for b in range(fourth.bit_length() - 1)]
     bits = [lax.rem(me // (fourth << b), 2) for b in range(PARTS.bit_length() - 1)]
 
     def part_copy(step, to):
         return pltpu.make_async_remote_copy(
             src_ref=part_ref.at[pl.ds(to * share, share)],
             dst_ref=got_part.at[step],
-            send_sem=part_send,
+            send_sem=send_sem,
             recv_sem=part_recv,
             device_id={"wide": to},
             device_id_type=MESH,
@@ -360,16 +371,15 @@
             part_ref[side * some + d] = jnp.concatenate(pieces, axis=1).astype(BF16)
         flipped = [1 - v if side >> b & 1 else v for b, v in enumerate(bits)]
         base = sum(v * (fourth << b) for b, v in enumerate(flipped))
-        for i in range(fourth - 1, 0, -1):
-            to = side * fourth + corner
-            for b, flip in enumerate(flips):
-                if i >> b & 1:
-                    to = to + flip
-            part_copy(base + i, to).start()
-
-        @pl.when(base > 0)
-        def _():
-            part_copy(base, side * fourth + corner).start()
+        for i in range(fourth):
+            to = side * fourth + i
+            slot = base
+            for b, v in enumerate(low_bits):
+                slot = slot + ((1 - v if i >> b & 1 else v) << b)
+
+            @pl.when(to != me)
+            def _():
+                part_copy(slot, to).start()
 
     col = lax.broadcasted_iota(jnp.int32, (8, LANES), 1)
     t_c, t_s = cos_sin_turns(((col % 8) * row8).astype(F32) * 0.125)
@@ -397,8 +407,7 @@
         per = window // LANES
         for p in range(per):
             out_ref[sub, pl.ds(p, 8, stride=per), :] = out[:, p * LANES : (p + 1) * LANES]
-    wait_all(got_power, power_send)
-    wait_all(got_part, part_send)
+    wait_all(got_part, send_sem)
 
 
 def body(n, filterbank, channel_mask, band_edges, dm_delays):
@@ -434,14 +443,14 @@
             pltpu.VMEM((PARTS * supers, local, LANES), BF16),
             pltpu.VMEM((PARTS * supers, local, LANES), BF16),
             pltpu.VMEM((8, local, window), BF16),
+            pltpu.VMEM((4, local, window), F32),
             pltpu.VMEM((8, samples // 256, 16, local), BF16),
             pltpu.VMEM((local, LANES), F32),
             pltpu.VMEM((1, LANES), F32),
             pltpu.VMEM((n, 1, LANES), F32),
             pltpu.VMEM((trials, 16, LANES), BF16),
             pltpu.VMEM((n, share, 16, LANES), BF16),
-            pltpu.SemaphoreType.DMA((3,)), pltpu.SemaphoreType.DMA((local // 64,)), pltpu.SemaphoreType.DMA((3,)),
-            dma, dma, dma, dma,
+            pltpu.SemaphoreType.DMA((3,)), dma, dma, dma, dma,
         ],
         compiler_params=pltpu.CompilerParams(
             collective_id=0, has_side_effects=True, vmem_limit_bytes=24 << 20

time: 18.3 us -> 18.1 us (0.989)
  Pallas kernels: 17.5 us -> 17.3 us
where the time goes in v3:
time: 18.1 us; the launch traced here: 18 us
  Pallas kernels  17.3 us (96%)
  local copies, waits for them, and re-layouts  0.61 us (3%)
    pallas_call x1, Pallas kernels, body(): pl.pallas_call(functools.partial(fused_kernel, n, bands, channels, trials...  17.3 us
    unnamed x1, local copies, waits for them, and re-layouts  0.61 us

profile of v3, /device:TPU:0, one launch (start us, length us, event | category | flops | bytes accessed | tf_op | source)
XLA Modules:
  0.0 18.0 jit_solution(1770382501393970397)
XLA Ops:
  0.0 17.3 %shard_map.73 = f32[1,32,128]{2,1,0:T(8,128)S(1)} custom-call(s32[7]{0:T(128)} %edges_hbm.1, s32[16]{0:T(128)} %delays_hbm.1, s32[1,256]{1,0:T(1,128)} %bitcast.5, bf16[256,4096]{1,0:T(8,128)(2,1)} %bitcast.4, bf16[2048,512]{1,0:T(8,128)(2,1)} %constant.6.clone.tab_hbm, bf16[256,1024]{1,0:T(8,128)(2,1)} %constant.7.clone.inv_hbm, ...), custom_call_target="tpu_custom_call" | custom-call | tf_op jit(solution)/shard_map/pallas_call | solution.py:427
  17.3 0.6 %copy.9 = f32[1,1,4096]{2,1,0:T(1,128)} copy(f32[1,1,4096]{2,1,0:T(1,128)S(1)} %bitcast.3) | data formatting | bytes 32768

commit v4 on v3

--- a/solution.py
+++ b/solution.py
@@ -340,30 +340,26 @@
         kept = []
         for block in range(supers):
             xa, xb = base_c[side * supers + block], base_s[side * supers + block]
-            got_re = got_im = jnp.zeros((8, LANES), F32)
+            got = [jnp.zeros((8, LANES), F32)] * 4
             for k in range(4):
                 c, s = rot_c[4 * side + k].astype(BF16), rot_s[4 * side + k].astype(BF16)
                 moving = jnp.concatenate(
                     [spec_ref[j, near * block + q] for j in (3 - k, 4 + k) for q in range(near)], axis=0
                 )
-                one = jnp.concatenate([c * xa, s * xb], axis=1)
-                two = jnp.concatenate([s * xa, c * xb], axis=1)
-                one = jnp.dot(moving, one, preferred_element_type=F32)
-                two = jnp.dot(moving, two, preferred_element_type=F32)
-                ac, bs, as_, bc = one[:, :LANES], one[:, LANES:], two[:, :LANES], two[:, LANES:]
-                for q in range(near):
-                    re = slice(16 * q, 16 * q + 8)
-                    im = slice(16 * q + 8, 16 * q + 16)
-                    out_re = (ac[re] + bs[re]) - (bc[im] - as_[im])
-                    out_im = (bc[re] - as_[re]) + (ac[im] + bs[im])
-                    got_re = jnp.where(code == 8 * q + 3 - k, out_re, got_re)
-                    got_im = jnp.where(code == 8 * q + 3 - k, out_im, got_im)
-                    re = slice(16 * (near + q), 16 * (near + q) + 8)
-                    im = slice(16 * (near + q) + 8, 16 * (near + q) + 16)
-                    out_re = (ac[re] - bs[re]) - (as_[im] + bc[im])
-                    out_im = (as_[re] + bc[re]) + (ac[im] - bs[im])
-                    got_re = jnp.where(code == 8 * q + 4 + k, out_re, got_re)
-                    got_im = jnp.where(code == 8 * q + 4 + k, out_im, got_im)
+                waves = [jnp.concatenate(v, axis=1) for v in ([c * xa, s * xb], [c * xb, s * xa])]
+                for w, wave in enumerate(waves):
+                    both = jnp.dot(moving, wave, preferred_element_type=F32)
+                    near_c, near_s = both[:, :LANES], both[:, LANES:]
+                    for q in range(2 * near):
+                        here = code == (8 * q + 3 - k if q < near else 8 * (q - near) + 4 + k)
+                        for part in range(2):
+                            at = slice(16 * q + 8 * part, 16 * q + 8 * part + 8)
+                            if (w == 0) == (q < near):
+                                value = near_c[at] + near_s[at]
+                            else:
+                                value = near_c[at] - near_s[at]
+                            got[2 * w + part] = jnp.where(here, value, got[2 * w + part])
+            got_re, got_im = got[0] - got[3], got[1] + got[2]
             kept.append(jnp.concatenate([got_re, got_im], axis=0))
         turned = jnp.transpose(jnp.concatenate(kept, axis=0))
         for d in range(some):

time: 18.1 us -> 18.1 us (level)
  no operation moved by 1% of the time
where the time goes in v4:
time: 18.1 us; the launch traced here: 17.9 us
  Pallas kernels  17.3 us (96%)
  local copies, waits for them, and re-layouts  0.61 us (3%)
    pallas_call x1, Pallas kernels, body(): pl.pallas_call(functools.partial(fused_kernel, n, bands, channels, trials...  17.3 us
    unnamed x1, local copies, waits for them, and re-layouts  0.61 us

profile of v4, /device:TPU:0, one launch (start us, length us, event | category | flops | bytes accessed | tf_op | source)
XLA Modules:
  0.0 17.9 jit_solution(2844528044285904882)
XLA Ops:
  0.0 17.3 %shard_map.73 = f32[1,32,128]{2,1,0:T(8,128)S(1)} custom-call(s32[7]{0:T(128)} %edges_hbm.1, s32[16]{0:T(128)} %delays_hbm.1, s32[1,256]{1,0:T(1,128)} %bitcast.5, bf16[256,4096]{1,0:T(8,128)(2,1)} %bitcast.4, bf16[2048,512]{1,0:T(8,128)(2,1)} %constant.6.clone.tab_hbm, bf16[256,1024]{1,0:T(8,128)(2,1)} %constant.7.clone.inv_hbm, ...), custom_call_target="tpu_custom_call" | custom-call | tf_op jit(solution)/shard_map/pallas_call | solution.py:423
  17.3 0.6 %copy.9 = f32[1,1,4096]{2,1,0:T(1,128)} copy(f32[1,1,4096]{2,1,0:T(1,128)S(1)} %bitcast.3) | data formatting | bytes 32768
